TPU v7x, 32 devices: a whole 2x2x4 slice. The times are simulated.
32 devices in a mesh: pair: 2 (over core), vcol: 16 (over z, y, x).
Axes of the slice: x: 2, y: 2, z: 4, core: 2. Of those that a mesh axis runs over, the one named last changes fastest.
Arguments:
- amplitudes: bfloat16 [1280, 4096], P('pair', 'vcol'), may hold values from -6 to 6
- tile_owner: int32 [32], replicated, may hold values from 0 to 31, each once
- integrals: bfloat16 [4096, 4096], P('pair', 'vcol'), may hold values from -0.125 to 0.125
- screening: int32 [20, 32, 32], P('pair'), may hold values 0 or 1
- occ_energy: float32 [1280], P('pair'), may hold values from -1 to -0.2
- virt_energy: float32 [4096], replicated, may hold values from 0.2 to 1
Outputs:
- residual: bfloat16 [1280, 4096], P('pair', 'vcol')
Inputs may be any that keep to these rules, and one draw needn't show every extreme that they name: `tile_owner`: each of the 32 tiles appears exactly once.
All inputs are finite; a program needn't handle non-finite values. No bound on the sum of `screening` on one device may be relied on, other than what follows from the above.
Results may differ from a plain program's by a relative error of at most 0.0036.
Values may be sent and summed in bfloat16 or wider, within the bound.
A program may use at most 64 MiB of HBM per device.

v0:
```python
import jax
import jax.numpy as jnp
from jax import lax
from jax.sharding import PartitionSpec as P

TILE = 128
PBLK = 64
KT_DEV = 2


def one_hot(indices, length):
    return (indices[:, None] == jnp.arange(length, dtype=jnp.int32)[None, :]).astype(jnp.float32)


def gather_rows(panel):
    return lax.all_gather(panel, "pair", axis=0, tiled=True)


def local(amplitudes, tile_owner, integrals, screening, occ_energy, virt_energy):
    pair_local = amplitudes.shape[0]
    tile_count = tile_owner.shape[0]
    width = KT_DEV * TILE
    block_count = pair_local // PBLK
    column = lax.axis_index("vcol")
    first_slot = column * KT_DEV
    owned_tiles = lax.dynamic_slice_in_dim(tile_owner, first_slot, KT_DEV, 0)
    screen_float = screening.astype(jnp.float32)
    natural_tiles = first_slot + jnp.arange(KT_DEV, dtype=jnp.int32)
    panel = gather_rows(integrals)
    picked = jnp.einsum("bct,jt->bcj", screen_float, one_hot(natural_tiles, tile_count))
    marks_slot = jnp.take(picked, tile_owner, axis=1).astype(jnp.bfloat16)
    panel_slot = jnp.take(panel.reshape(tile_count, TILE, width), tile_owner, axis=0)
    piece_in = lax.all_gather(amplitudes, "vcol", axis=1, tiled=True)
    tiles_in = piece_in.shape[1] // TILE
    left_all = piece_in.reshape(block_count, PBLK, tiles_in * TILE)

    def one_block(operands):
        left_rows, marks = operands
        masked = (
            panel_slot.reshape(tiles_in, TILE, KT_DEV, TILE) * marks[:, None, :, None]
        ).reshape(tiles_in * TILE, width)
        return jnp.dot(left_rows, masked, preferred_element_type=jnp.float32)

    summed = lax.map(one_block, (left_all, marks_slot))
    ladder_local = summed.reshape(pair_local, width).astype(jnp.bfloat16)
    piece_in = lax.all_gather(ladder_local, "vcol", axis=1, tiled=True)
    tiles_in = piece_in.shape[1] // TILE
    chooser = one_hot(owned_tiles, tiles_in).astype(jnp.bfloat16)
    shaped = piece_in.reshape(piece_in.shape[0], tiles_in, TILE)
    ladder_owned = jnp.einsum(
        "pmk,jm->pjk", shaped, chooser, preferred_element_type=jnp.float32
    ).reshape(pair_local, width)
    virt_owned = jnp.dot(
        one_hot(owned_tiles, tile_count),
        virt_energy.reshape(tile_count, TILE),
        precision=lax.Precision.HIGHEST,
    ).reshape(width)
    residual = ladder_owned + (virt_owned[None, :] - occ_energy[:, None]) * amplitudes.astype(
        jnp.float32
    )
    return residual.astype(jnp.bfloat16)


def solution(mesh):
    return jax.shard_map(
        local,
        mesh=mesh,
        in_specs=(P("pair", "vcol"), P(), P("pair", "vcol"), P("pair", None, None), P("pair"), P()),
        out_specs=P("pair", "vcol"),
        check_vma=False,
    )
```

profile of v0, /device:TPU:0, one launch (start us, length us, event | category | flops | bytes accessed | tf_op | source)
XLA Modules:
  0.0 258.9 jit_solution(7271926033626075725)
XLA Ops:
  6.5 0.7 all-gather.6.cloned.1.call-update
  7.3 0.7 all-gather.4.cloned.1.call-update
  8.1 1.2 convolution_bitcast_fusion.1
  9.2 0.1 copy.9
  9.4 0.7 compare_select_fusion
  10.1 0.6 gather_fusion
  10.7 0.7 compare_and_fusion
  11.3 0.1 fusion.8
  11.5 10.7 %all-gather.6.cloned.1.call-done = bf16[4096,256]{1,0:T(8,128)(2,1)} async-done(((bf16[2048,256]{1,0:T(8,128)(2,1)}), bf16[4096,256]{1,0:T(8,128)(2,1)}) %all-gather.6.cloned.1.call-update) | async-done | bytes 2097168 | tf_op jit(solution)/shard_map/all_gather | solution.py:16
  22.2 3.7 %gather_fusion.1 = bf16[32,128,256]{2,1,0:T(8,128)(2,1)} fusion(bf16[32,128,256]{2,1,0:T(8,128)(2,1)} %bitcast.60, s32[1024]{0:T(1024)S(1)} %pad_clamp_fusion), kind=kCustom, calls=%fused_computation.1 | custom fusion | bytes 4194432 | tf_op jit(solution)/shard_map/jit(_take)/gather | solution.py:32
  25.9 1.8 broadcast_select_fusion
  27.7 96.8 %all-gather.4.cloned.1.call-done = bf16[640,4096]{1,0:T(8,128)(2,1)} async-done(((bf16[640,256]{1,0:T(8,128)(2,1)}), bf16[640,4096]{1,0:T(8,128)(2,1)}) %all-gather.4.cloned.1.call-update) | async-done | bytes 5242896 | tf_op jit(solution)/shard_map/all_gather | solution.py:33
  124.5 25.2 %while.10 = (s32[]{:T(128)}, bf16[10,64,256]{2,1,0:T(8,128)(2,1)}, bf16[10,64,4096]{2,1,0:T(8,128)(2,1)}, bf16[10,32,2]{1,2,0:T(2,128)(2,1)S(1)}, bf16[32,128,256]{2,1,0:T(8,128)(2,1)S(1)}, /*index=5*/s32[]{:T(128)}) while((s32[]{:T(128)}, bf16[10,64,256]{2,1,0:T(8,128)(2,1)}, bf16[10,64,4096]{2,1,0:T(8,128)(2,1)}, ...), condition=%wide.region_1.2_spmd, body=%wide.region_0.1_spmd.sunk | while | flops 135266304 | bytes 6948553 | solution.py:44
  124.5 0.1 copy.19
  124.7 0.1 broadcast_multiply_fusion.2
  124.9 2.1 fusion.27
  127.0 0.1 copy.19
  127.2 0.1 broadcast_multiply_fusion.2
  127.4 2.1 fusion.27
  129.5 0.1 copy.19
  129.8 0.1 broadcast_multiply_fusion.2
  129.9 2.1 fusion.27
  132.1 0.1 copy.19
  132.3 0.1 broadcast_multiply_fusion.2
  132.4 2.1 fusion.27
  134.6 0.1 copy.19
  134.8 0.1 broadcast_multiply_fusion.2
  135.0 2.1 fusion.27
  137.1 0.1 copy.19
  137.3 0.1 broadcast_multiply_fusion.2
  137.5 2.1 fusion.27
  139.6 0.1 copy.19
  139.8 0.1 broadcast_multiply_fusion.2
  140.0 2.1 fusion.27
  142.1 0.1 copy.19
  142.4 0.1 broadcast_multiply_fusion.2
  142.5 2.1 fusion.27
  144.6 0.1 copy.19
  144.9 0.1 broadcast_multiply_fusion.2
  145.0 2.1 fusion.27
  147.2 0.1 copy.19
  147.4 0.1 broadcast_multiply_fusion.2
  147.5 2.1 fusion.27
  149.8 0.2 convolution_bitcast_fusion.2
  150.0 96.4 %all-gather.8.cloned.1.call-done = bf16[640,4096]{1,0:T(8,128)(2,1)} async-done(((bf16[640,256]{1,0:T(8,128)(2,1)}), bf16[640,4096]{1,0:T(8,128)(2,1)}) %all-gather.8.cloned.1.call-update) | async-done | bytes 5242896 | tf_op jit(solution)/shard_map/all_gather | solution.py:46
  246.4 4.1 %copy.12 = bf16[80,8,32,128]{3,2,1,0:T(8,128)(2,1)S(1)} copy(bf16[80,8,32,128]{3,1,2,0:T(8,128)(2,1)} %bitcast.58) | data formatting | bytes 10485760
  250.6 0.9 fusion.13
  251.5 0.9 fusion.5
  (47 shorter events, 1.5 us)
Async XLA Ops:
  6.5 143.3 %copy-start = (f32[4096]{0:T(1024)S(1)}, f32[4096]{0:T(1024)}, u32[]{:S(2)}) copy-start(f32[4096]{0:T(1024)} %param.13) | copy-start | bytes 49156
  6.5 15.7 %all-gather.6.cloned.1.call-start = ((), (), s32[]{:S(2)}) async-start(), calls=%async_computation.1 | async-start | bytes 3145728 | tf_op jit(solution)/shard_map/all_gather | solution.py:16
  7.3 117.2 %all-gather.4.cloned.1.call-start = ((), (), s32[]{:S(2)}) async-start(), calls=%async_computation | async-start | bytes 5570560 | tf_op jit(solution)/shard_map/all_gather | solution.py:33
  8.0 238.4 %all-gather.8.cloned.1.call-start = ((), (), s32[]{:S(2)}) async-start(), calls=%async_computation.2 | async-start | bytes 5570560 | tf_op jit(solution)/shard_map/all_gather | solution.py:46
  124.5 25.2 %copy-start.3 = (s32[32]{0:T(128)S(1)}, s32[32]{0:T(128)}, u32[]{:S(2)}) copy-start(s32[32]{0:T(128)} %param.9) | copy-start | bytes 388
  250.5 1.0 copy-start.1
  250.5 1.0 copy-start.2
Sparse Core Ops, SparseCore 0:
  8.9 13.2 all-gather.5
  24.9 99.5 all-gather.3
  149.8 96.5 all-gather.7
where the time goes:
time: 260 us; the launch traced here: 259 us
  waiting for transfers between devices  205 us (79%)
  matrix products  23.6 us (9%)
  between operations  13.2 us (5%)
  local copies, waits for them, and re-layouts  10.9 us (4%)
  other arithmetic  5.66 us (2%)
    all_gather x1, waiting for transfers between devices, local(): piece_in = lax.all_gather(amplitudes, 'vcol', axis=1, tiled=True)  96.8 us
    all_gather x1, waiting for transfers between devices, local(): piece_in = lax.all_gather(ladder_local, 'vcol', axis=1, tiled=True)  96.4 us
    dot_general x10, matrix products, one_block(): return jnp.dot(left_rows, masked, preferred_element_type=jnp.float32)  21.4 us
    all_gather x1, waiting for transfers between devices, gather_rows(): return lax.all_gather(panel, 'pair', axis=0, tiled=True)  10.7 us
  transfers between devices with their start and end apart: 3, of which 3 were waited for; matrix products, arithmetic and copies ran while one was open for 4% of the time, Pallas kernels for 0%

commit v1 on v0

--- a/solution.py
+++ b/solution.py
@@ -30,7 +30,8 @@
     picked = jnp.einsum("bct,jt->bcj", screen_float, one_hot(natural_tiles, tile_count))
     marks_slot = jnp.take(picked, tile_owner, axis=1).astype(jnp.bfloat16)
     panel_slot = jnp.take(panel.reshape(tile_count, TILE, width), tile_owner, axis=0)
-    piece_in = lax.all_gather(amplitudes, "vcol", axis=1, tiled=True)
+    parts = lax.all_gather(amplitudes, "vcol", axis=0, tiled=False)
+    piece_in = jnp.concatenate(parts, axis=1)
     tiles_in = piece_in.shape[1] // TILE
     left_all = piece_in.reshape(block_count, PBLK, tiles_in * TILE)
 

time: 260 us -> 263 us (1.012)
  local copies, waits for them, and re-layouts: 10.9 us -> 27.6 us
  waiting for transfers between devices: 205 us -> 192 us
    all_gather x1, waiting for transfers between devices: 96.8 us -> 82.8 us  [local(): parts = lax.all_gather(amplitudes, 'vcol', axis=0, tiled=False)]
    another operation x0 -> x1, local copies, waits for them, and re-layouts: none -> 8.92 us  [local(): left_all = piece_in.reshape(block_count, PBLK, tiles_in * TILE)]
    all_gather x0 -> x1, local copies, waits for them, and re-layouts: none -> 7.79 us  [local(): parts = lax.all_gather(amplitudes, 'vcol', axis=0, tiled=False)]
where the time goes in v1:
time: 263 us; the launch traced here: 262 us
  waiting for transfers between devices  192 us (73%)
  local copies, waits for them, and re-layouts  27.6 us (10%)
  matrix products  23.5 us (9%)
  between operations  13.2 us (5%)
  other arithmetic  5.66 us (2%)
    all_gather x1, waiting for transfers between devices, local(): piece_in = lax.all_gather(ladder_local, 'vcol', axis=1, tiled=True)  97 us
    all_gather x1, waiting for transfers between devices, local(): parts = lax.all_gather(amplitudes, 'vcol', axis=0, tiled=False)  82.8 us
    dot_general x10, matrix products, one_block(): return jnp.dot(left_rows, masked, preferred_element_type=jnp.float32)  21.4 us
    all_gather x1, waiting for transfers between devices, gather_rows(): return lax.all_gather(panel, 'pair', axis=0, tiled=True)  10.7 us
    another operation x1, local copies, waits for them, and re-layouts, local(): left_all = piece_in.reshape(block_count, PBLK, tiles_in * TILE)  8.92 us
    all_gather x1, local copies, waits for them, and re-layouts, local(): parts = lax.all_gather(amplitudes, 'vcol', axis=0, tiled=False)  7.79 us
  transfers between devices with their start and end apart: 3, of which 3 were waited for; matrix products, arithmetic and copies ran while one was open for 4% of the time, Pallas kernels for 0%

profile of v1, /device:TPU:0, one launch (start us, length us, event | category | flops | bytes accessed | tf_op | source)
XLA Modules:
  0.0 262.2 jit_solution(3415628741420785148)
XLA Ops:
  6.5 0.7 all-gather.5.cloned.1.call-update
  7.3 0.7 all-gather.9.cloned.1.call-update
  8.1 1.2 convolution_bitcast_fusion.1
  9.2 0.1 copy.11
  9.4 0.7 compare_select_fusion
  10.0 0.6 gather_fusion
  10.6 0.7 compare_and_fusion
  11.5 10.7 %all-gather.5.cloned.1.call-done = bf16[4096,256]{1,0:T(8,128)(2,1)} async-done(((bf16[2048,256]{1,0:T(8,128)(2,1)}), bf16[4096,256]{1,0:T(8,128)(2,1)}) %all-gather.5.cloned.1.call-update) | async-done | bytes 2097168 | tf_op jit(solution)/shard_map/all_gather | solution.py:16
  22.2 3.7 %gather_fusion.1 = bf16[32,128,256]{2,1,0:T(8,128)(2,1)} fusion(bf16[32,128,256]{2,1,0:T(8,128)(2,1)} %bitcast.65, s32[1024]{0:T(1024)S(1)} %pad_clamp_fusion), kind=kCustom, calls=%fused_computation.1 | custom fusion | bytes 4194432 | tf_op jit(solution)/shard_map/jit(_take)/gather | solution.py:32
  25.9 1.8 broadcast_select_fusion
  27.7 82.8 %all-gather.9.cloned.1.call-done = bf16[10240,256]{1,0:T(8,128)(2,1)} async-done(((bf16[640,256]{1,0:T(8,128)(2,1)}), bf16[10240,256]{1,0:T(8,128)(2,1)}) %all-gather.9.cloned.1.call-update) | async-done | bytes 5242896 | tf_op jit(solution)/shard_map/all_gather | solution.py:33
  110.5 7.8 %copy.20 = bf16[16,640,256]{2,0,1:T(8,128)(2,1)} copy(bf16[16,640,256]{2,1,0:T(8,128)(2,1)} %bitcast.62) | data formatting | bytes 10485760 | tf_op jit(solution)/shard_map/all_gather | solution.py:33
  118.3 8.9 %reshape_reshape.3 = bf16[10,64,4096]{2,1,0:T(8,128)(2,1)} reshape(bf16[640,16,256]{2,1,0:T(8,128)(2,1)} %bitcast.61) | data formatting | bytes 10485760 | tf_op jit(solution)/shard_map/reshape;reshape | solution.py:36
  127.2 25.2 %while.10 = (s32[]{:T(128)}, bf16[10,64,256]{2,1,0:T(8,128)(2,1)}, bf16[10,64,4096]{2,1,0:T(8,128)(2,1)}, bf16[10,32,2]{1,2,0:T(2,128)(2,1)S(1)}, bf16[32,128,256]{2,1,0:T(8,128)(2,1)S(1)}, /*index=5*/s32[]{:T(128)}) while((s32[]{:T(128)}, bf16[10,64,256]{2,1,0:T(8,128)(2,1)}, bf16[10,64,4096]{2,1,0:T(8,128)(2,1)}, ...), condition=%wide.region_1.2_spmd, body=%wide.region_0.1_spmd.sunk | while | flops 135266304 | bytes 6948561 | solution.py:45
  127.2 0.1 copy.23
  127.4 0.1 broadcast_multiply_fusion.2
  127.6 2.1 fusion.27
  129.7 0.1 copy.23
  129.9 0.1 broadcast_multiply_fusion.2
  130.1 2.1 fusion.27
  132.2 0.1 copy.23
  132.5 0.1 broadcast_multiply_fusion.2
  132.6 2.1 fusion.27
  134.7 0.1 copy.23
  135.0 0.1 broadcast_multiply_fusion.2
  135.1 2.1 fusion.27
  137.3 0.1 copy.23
  137.5 0.1 broadcast_multiply_fusion.2
  137.6 2.1 fusion.27
  139.8 0.1 copy.23
  140.0 0.1 broadcast_multiply_fusion.2
  140.2 2.1 fusion.27
  142.3 0.1 copy.23
  142.5 0.1 broadcast_multiply_fusion.2
  142.7 2.1 fusion.27
  144.8 0.1 copy.23
  145.0 0.1 broadcast_multiply_fusion.2
  145.2 2.1 fusion.27
  147.3 0.1 copy.23
  147.6 0.1 broadcast_multiply_fusion.2
  147.7 2.1 fusion.27
  150.1 0.1 broadcast_multiply_fusion.2
  150.2 2.1 fusion.27
  152.5 0.2 convolution_bitcast_fusion.2
  152.7 97.0 %all-gather.7.cloned.1.call-done = bf16[640,4096]{1,0:T(8,128)(2,1)} async-done(((bf16[640,256]{1,0:T(8,128)(2,1)}), bf16[640,4096]{1,0:T(8,128)(2,1)}) %all-gather.7.cloned.1.call-update) | async-done | bytes 5242896 | tf_op jit(solution)/shard_map/all_gather | solution.py:47
  249.6 4.1 %copy.14 = bf16[80,8,32,128]{3,2,1,0:T(8,128)(2,1)S(1)} copy(bf16[80,8,32,128]{3,1,2,0:T(8,128)(2,1)} %bitcast.63) | data formatting | bytes 10485760
  253.8 0.9 fusion.13
  254.7 0.9 fusion.5
  (49 shorter events, 1.7 us)
Async XLA Ops:
  6.5 145.9 %copy-start = (f32[4096]{0:T(1024)S(1)}, f32[4096]{0:T(1024)}, u32[]{:S(2)}) copy-start(f32[4096]{0:T(1024)} %param.13) | copy-start | bytes 49156
  6.5 15.7 %all-gather.5.cloned.1.call-start = ((), (), s32[]{:S(2)}) async-start(), calls=%async_computation | async-start | bytes 3145728 | tf_op jit(solution)/shard_map/all_gather | solution.py:16
  7.3 103.2 %all-gather.9.cloned.1.call-start = ((), (), s32[]{:S(2)}) async-start(), calls=%async_computation.2 | async-start | bytes 5570560 | tf_op jit(solution)/shard_map/all_gather | solution.py:33
  8.0 241.6 %all-gather.7.cloned.1.call-start = ((), (), s32[]{:S(2)}) async-start(), calls=%async_computation.1 | async-start | bytes 5570560 | tf_op jit(solution)/shard_map/all_gather | solution.py:47
  127.2 25.2 %copy-start.3 = (s32[32]{0:T(128)S(1)}, s32[32]{0:T(128)}, u32[]{:S(2)}) copy-start(s32[32]{0:T(128)} %param.9) | copy-start | bytes 388
  253.8 1.0 copy-start.1
  253.8 1.0 copy-start.2
Sparse Core Ops, SparseCore 0:
  8.9 13.2 all-gather.4
  25.0 85.4 all-gather.8
  152.5 97.0 all-gather.6
